TPU v7x, 512 devices: a whole 4x8x8 slice. The times are simulated.
512 devices in a mesh: gx: 16 (over y, core), gy: 32 (over z, x).
Axes of the slice: x: 4, y: 8, z: 8, core: 2. Of those that a mesh axis runs over, the one named last changes fastest.
Arguments:
- inputs: bfloat16 [256, 4, 2304], P('gy', None, 'gx'), may hold values from -8 to 8
- cache_pool: bfloat16 [2, 64, 4096, 1024], P(None, 'gx', 'gy'), may hold values from -6 to 6
- lengths: int32 [32], P('gy'), may hold values from 1 to 32768, as said below
- block_table: int32 [32, 33], P('gy'), may hold values from -1 to 63, as said below
- parents: int32 [3, 256], P(None, 'gy'), may hold values from 0 to 7
- norm_gains: float32 [4, 2304], P(None, 'gx'), may hold values from -0.5 to 1
- w_query: bfloat16 [2304, 2048], P('gx', 'gy'), may hold values from -0.125 to 0.125
- w_key: bfloat16 [2304, 1024], P('gx', 'gy'), may hold values from -0.125 to 0.125
- w_value: bfloat16 [2304, 1024], P('gx', 'gy'), may hold values from -0.125 to 0.125
- w_out: bfloat16 [2048, 2304], P('gy', 'gx'), may hold values from -1 to 1
- w_gate: bfloat16 [2304, 9216], P('gx', 'gy'), may hold values from -0.125 to 0.125
- w_up: bfloat16 [2304, 9216], P('gx', 'gy'), may hold values from -0.125 to 0.125
- w_down: bfloat16 [9216, 2304], P('gy', 'gx'), may hold values from -1 to 1
Outputs:
- outputs: bfloat16 [256, 4, 2304], P('gy', None, 'gx')
Inputs may be any that keep to these rules, and one draw needn't show every extreme that they name: `lengths`: a group's beams share its prompt length. block_table[g, j] is the slot, numbered over the index of gy that holds group g as gx index times 4 plus the device's slot, of page first(g) + j of the group, for j up to (lengths[g] - 1) // 128 - first(g), and -1 beyond; no slot is named twice; a device holds at most 4 pages, and some device holds 4. Beam b at step s + 1 continues beam parents[s, b] of its own group, numbered within the group.
All inputs are finite; a program needn't handle non-finite values.
Results may differ from a plain program's by a relative error of at most 0.015.
Values may be sent and summed in bfloat16 or wider, within the bound.
A program may use at most 64 MiB of HBM per device.

v0:
```python
import jax
import jax.numpy as jnp
from jax import lax
from jax.sharding import PartitionSpec as P

D = 2304
HEADS = 8
KV_HEADS = 4
HEAD_DIM = 256
WINDOW = 4096
PAGE = 128
BEAM = 8
EPSILON = 1e-06
SOFT_CAP = 50.0
ROPE_BASE = 10000.0


def rotate(values, positions):
    half_width = values.shape[-1] // 2
    inverse_freq = ROPE_BASE ** (
        -jnp.arange(half_width, dtype=jnp.float32) * 2.0 / values.shape[-1]
    )
    angles = positions[..., None].astype(jnp.float32) * inverse_freq
    cosine = jnp.cos(angles)[..., None, :]
    sine_part = jnp.sin(angles)[..., None, :]
    first_half = values[..., :half_width]
    second_half = values[..., half_width:]
    return jnp.concatenate(
        [
            first_half * cosine - second_half * sine_part,
            second_half * cosine + first_half * sine_part,
        ],
        axis=-1,
    )


def ancestry(parents, beam_count, group_size, steps_count):
    beam_ids = jnp.arange(beam_count, dtype=jnp.int32)
    group_base = beam_ids // group_size * group_size
    table_rows = []
    for moment in range(steps_count):
        current = beam_ids
        chain_list = [beam_ids] * steps_count
        for earlier in range(moment, 0, -1):
            current = group_base + jnp.take(parents[earlier - 1], current)
            chain_list[earlier - 1] = current
        table_rows.append(jnp.stack(chain_list))
    return jnp.stack(table_rows)


def tail_terms(grouped, key_steps, value_steps, ancestors):
    steps_count = grouped.shape[1]
    step_ids = jnp.arange(steps_count, dtype=jnp.int32)
    tail_keys = key_steps[ancestors, step_ids[None, :, None]]
    tail_values = value_steps[ancestors, step_ids[None, :, None]]
    scores = jnp.einsum(
        "bskgd,sjbkd->bskgj", grouped, tail_keys, preferred_element_type=jnp.float32
    )
    allowed = step_ids[None, :] <= step_ids[:, None]
    weights = jnp.where(
        allowed[None, :, None, None, :], jnp.exp(SOFT_CAP * jnp.tanh(scores / SOFT_CAP)), 0.0
    )
    numerator = jnp.einsum(
        "bskgj,sjbkd->bskgd",
        weights.astype(jnp.bfloat16),
        tail_values,
        preferred_element_type=jnp.float32,
    )
    return (numerator, jnp.sum(weights, axis=-1))


def body(
    inputs,
    cache_pool,
    lengths,
    block_table,
    parents,
    norm_gains,
    w_query,
    w_key,
    w_value,
    w_out,
    w_gate,
    w_up,
    w_down,
):
    col_beams, steps_count, width_part = inputs.shape
    group_count = lengths.shape[0]
    slot_count = cache_pool.shape[1]
    rep_heads = HEADS // KV_HEADS
    x_wide = inputs.astype(jnp.float32)
    gain_rows = 1.0 + norm_gains
    square_sum = lax.psum(jnp.sum(x_wide * x_wide, axis=-1), "gx")
    normed_share = (x_wide * lax.rsqrt(square_sum / D + EPSILON)[..., None] * gain_rows[0]).astype(
        jnp.bfloat16
    )
    normed = lax.all_gather(normed_share, "gy", axis=0, tiled=True)
    all_beams = normed.shape[0]
    flat_rows = normed.reshape(-1, width_part)

    def project(weight):
        return jnp.dot(flat_rows, weight, preferred_element_type=jnp.float32).reshape(
            all_beams, steps_count, weight.shape[1]
        )

    query_sum, key_sum, value_sum = lax.psum(
        (project(w_query), project(w_key), project(w_value)), "gx"
    )
    query_raw, key_raw, value_raw = (
        lax.all_to_all(query_sum, "gy", split_axis=0, concat_axis=2, tiled=True),
        lax.all_to_all(key_sum, "gy", split_axis=0, concat_axis=2, tiled=True),
        lax.all_to_all(value_sum, "gy", split_axis=0, concat_axis=2, tiled=True),
    )
    beam_lengths = jnp.repeat(lengths, BEAM)
    step_ids = jnp.arange(steps_count, dtype=jnp.int32)
    positions = beam_lengths[:, None] + step_ids[None, :]
    queries = (
        rotate(query_raw.reshape(col_beams, steps_count, HEADS, HEAD_DIM), positions)
        * HEAD_DIM ** (-0.5)
    ).astype(jnp.bfloat16)
    key_steps = rotate(
        key_raw.reshape(col_beams, steps_count, KV_HEADS, HEAD_DIM), positions
    ).astype(jnp.bfloat16)
    value_steps = value_raw.reshape(col_beams, steps_count, KV_HEADS, HEAD_DIM).astype(jnp.bfloat16)
    grouped = queries.reshape(col_beams, steps_count, KV_HEADS, rep_heads, HEAD_DIM)
    slot_ids = lax.axis_index("gx") * slot_count + jnp.arange(slot_count, dtype=jnp.int32)
    matches = block_table[:, :, None] == slot_ids[None, None, :]
    owner_mask = jnp.any(matches, axis=1)
    slot_used = jnp.any(owner_mask, axis=0)
    page_number = jnp.sum(
        jnp.where(matches, jnp.arange(block_table.shape[1], dtype=jnp.int32)[None, :, None], 0),
        axis=(0, 1),
    )
    first_page = jnp.maximum(lengths - WINDOW + 1, 0) // PAGE
    slot_first = jnp.sum(jnp.where(owner_mask, first_page[:, None], 0), axis=0)
    slot_length = jnp.sum(jnp.where(owner_mask, lengths[:, None], 0), axis=0)
    key_positions = (slot_first + page_number)[:, None] * PAGE + jnp.arange(PAGE, dtype=jnp.int32)[
        None, :
    ]
    group_queries = grouped.reshape(group_count, BEAM, steps_count, KV_HEADS, rep_heads, HEAD_DIM)
    slot_queries = jnp.einsum(
        "an,abskgd->nbskgd",
        owner_mask.astype(jnp.bfloat16),
        group_queries,
        preferred_element_type=jnp.float32,
    ).astype(jnp.bfloat16)
    page_keys = cache_pool[0].reshape(slot_count, PAGE, KV_HEADS, HEAD_DIM)
    page_values = cache_pool[1].reshape(slot_count, PAGE, KV_HEADS, HEAD_DIM)
    scores = jnp.einsum(
        "nbskgd,ntkd->nbskgt", slot_queries, page_keys, preferred_element_type=jnp.float32
    )
    lower_bound = slot_length[:, None] + step_ids[None, :] - WINDOW + 1
    visible = (
        slot_used[:, None, None]
        & (key_positions[:, None, :] < slot_length[:, None, None])
        & (key_positions[:, None, :] >= lower_bound[:, :, None])
    )
    weights = jnp.where(
        visible[:, None, :, None, None, :], jnp.exp(SOFT_CAP * jnp.tanh(scores / SOFT_CAP)), 0.0
    )
    page_den = jnp.sum(weights, axis=-1)
    page_num = jnp.einsum(
        "nbskgt,ntkd->nbskgd",
        weights.astype(jnp.bfloat16),
        page_values,
        preferred_element_type=jnp.float32,
    )
    owner_wide = owner_mask.astype(jnp.float32)
    group_num = jnp.sum(owner_wide[:, :, None, None, None, None, None] * page_num[None], axis=1)
    group_den = jnp.sum(owner_wide[:, :, None, None, None, None] * page_den[None], axis=1)
    total_num, total_den = lax.psum((group_num, group_den), "gx")
    ancestors = ancestry(parents, col_beams, BEAM, steps_count)
    tail_num, tail_den = tail_terms(grouped, key_steps, value_steps, ancestors)
    numerator = total_num.reshape(col_beams, steps_count, KV_HEADS, rep_heads, HEAD_DIM) + tail_num
    denominator = total_den.reshape(col_beams, steps_count, KV_HEADS, rep_heads) + tail_den
    attended = (
        (numerator / denominator[..., None])
        .astype(jnp.bfloat16)
        .reshape(col_beams, steps_count, HEADS * HEAD_DIM)
    )
    head_rows = lax.all_to_all(attended, "gy", split_axis=2, concat_axis=0, tiled=True)
    head_width = head_rows.shape[2]
    attn_part = jnp.dot(
        head_rows.reshape(-1, head_width), w_out, preferred_element_type=jnp.float32
    ).reshape(all_beams, steps_count, width_part)
    attn_full = lax.psum(attn_part, "gy")
    residual = lax.all_gather(inputs, "gy", axis=0, tiled=True).astype(jnp.float32)
    attn_square = lax.psum(jnp.sum(attn_full * attn_full, axis=-1), "gx")
    mixed_full = (
        residual + attn_full * lax.rsqrt(attn_square / D + EPSILON)[..., None] * gain_rows[1]
    )
    mixed_square = lax.psum(jnp.sum(mixed_full * mixed_full, axis=-1), "gx")
    ff_input = (
        mixed_full * lax.rsqrt(mixed_square / D + EPSILON)[..., None] * gain_rows[2]
    ).astype(jnp.bfloat16)
    mixed_rows = lax.dynamic_slice_in_dim(
        mixed_full, lax.axis_index("gy") * col_beams, col_beams, 0
    )
    gate_width = w_gate.shape[1]
    matrix_rows = ff_input.reshape(-1, width_part)
    gate_and_up = jnp.concatenate(
        [
            jnp.dot(matrix_rows, w_gate, preferred_element_type=jnp.float32),
            jnp.dot(matrix_rows, w_up, preferred_element_type=jnp.float32),
        ],
        axis=1,
    )
    activate_gate_and_up = lax.psum_scatter(
        gate_and_up.reshape(ff_input.shape[0], steps_count, 2 * gate_width),
        "gx",
        scatter_dimension=0,
        tiled=True,
    )
    hidden_share = (
        jax.nn.gelu(activate_gate_and_up[..., :gate_width], approximate=True)
        * activate_gate_and_up[..., gate_width:]
    ).astype(jnp.bfloat16)
    hidden_rows = lax.all_gather(hidden_share, "gx", axis=0, tiled=True)
    down_part = jnp.dot(
        hidden_rows.reshape(-1, gate_width), w_down, preferred_element_type=jnp.float32
    ).reshape(hidden_rows.shape[0], steps_count, width_part)
    down_own = lax.psum_scatter(down_part, "gy", scatter_dimension=0, tiled=True)
    out_square = lax.psum(jnp.sum(down_own * down_own, axis=-1), "gx")
    return (
        mixed_rows + down_own * lax.rsqrt(out_square / D + EPSILON)[..., None] * gain_rows[3]
    ).astype(jnp.bfloat16)


def solution(mesh):
    return jax.shard_map(
        body,
        mesh=mesh,
        in_specs=(
            P("gy", None, "gx"),
            P(None, "gx", "gy", None),
            P("gy"),
            P("gy", None),
            P(None, "gy"),
            P(None, "gx"),
            P("gx", "gy"),
            P("gx", "gy"),
            P("gx", "gy"),
            P("gy", "gx"),
            P("gx", "gy"),
            P("gx", "gy"),
            P("gy", "gx"),
        ),
        out_specs=P("gy", None, "gx"),
        check_vma=False,
    )
```

profile of v0, /device:TPU:1, one launch (start us, length us, event | category | flops | bytes accessed | tf_op | source)
XLA Modules:
  0.0 937.1 jit_solution(2836527621570253802)
XLA Ops:
  6.5 0.7 broadcast_add_fusion
  7.3 0.8 fusion.33
  8.1 29.8 %psum.70 = f32[8,4]{0,1:T(4,128)S(1)} all-reduce(f32[8,4]{0,1:T(4,128)S(1)} %fusion.33), channel_id=1, replica_groups=mesh['gx'=16,'gy'=32] {'gx'}, use_global_device_ids=true, to_apply=%region_3.0 | all-reduce | flops 32 | bytes 256 | tf_op jit(solution)/shard_map/psum | solution.py:93
  37.8 0.8 fusion.35
  38.6 36.1 %all_gather.10 = bf16[256,4,144]{2,0,1:T(8,128)(2,1)S(1)} all-gather(bf16[8,4,144]{2,0,1:T(8,128)(2,1)S(1)} %fusion.35), channel_id=1, replica_groups=mesh['gx'=16,'gy'=32] {'gy'}, dimensions={0}, use_global_device_ids=true | all-gather | bytes 304128 | tf_op jit(solution)/shard_map/all_gather | solution.py:97
  74.7 1.7 fusion.37
  76.5 0.8 compare_reduce_fusion
  77.4 0.8 fusion.49
  79.1 1.8 fusion.65
  80.9 0.6 gather_fusion.3
  81.6 0.6 gather_fusion.5
  82.2 0.6 gather_fusion.6
  82.9 0.6 gather_fusion.7
  83.6 0.6 gather_fusion.4
  84.6 111.0 %all-reduce.9.cloned.1.call-done = f32[256,4,64]{0,2,1:T(8,128)} async-done(((f32[256,4,64]{0,2,1:T(8,128)}), f32[256,4,64]{0,2,1:T(8,128)}) %all-reduce.9.cloned.1.call-update) | async-done | bytes 262160 | tf_op jit(solution)/shard_map/psum | solution.py:106
  195.6 1.2 copy.204
  196.8 1.2 reshape.614
  198.0 9.9 %all-to-all-start = ((f32[32,1,2048]{2,1,0:T(1,128)}), f32[32,1,2048]{2,1,0:T(1,128)S(1)}, u32[]{:S(2)}, u32[]{:S(2)}) async-start(f32[32,1,2048]{2,1,0:T(1,128)} %reshape.614), calls=%async_computation | async-start | bytes 524288 | tf_op jit(solution)/shard_map/all_to_all | solution.py:110
  207.9 0.6 gather_fusion.2
  208.5 1.3 copy.253
  209.9 0.7 copy.254
  210.7 0.9 fusion.44
  211.6 7.5 all-to-all-done
  219.6 1.3 reduce.5
  221.9 1.7 fusion.67
  224.1 0.8 copy.281
  225.1 47.4 %all-reduce.16 = (bf16[256,4,32]{0,2,1:T(8,128)(2,1)S(1)}, f32[8,4,4,2]{0,2,3,1:T(4,128)S(1)}) all-reduce(f32[256,4,32]{0,2,1:T(8,128)S(1)} %fusion.42, f32[8,4,4,2]{0,2,3,1:T(4,128)S(1)} %copy.223), channel_id=1, replica_groups=mesh['gx'=16,'gy'=32] {'gx'}, use_global_device_ids=true, to_apply=%region_8.10 | all-reduce | flops 33024 | bytes 198656 | tf_op jit(solution)/shard_map/psum | solution.py:106
  272.6 0.8 reshape.616
  273.5 3.8 all-to-all-start.2
  277.4 0.7 all-reduce.15.cloned.1.call-update
  278.1 120.2 %all-reduce.15.cloned.1.call-done = (f32[8,4,4,2,256]{4,3,2,1,0:T(2,128)}, f32[256,4,32]{0,2,1:T(8,128)}) async-done(((f32[8,4,4,2,256]{4,3,2,1,0:T(2,128)}, f32[256,4,32]{0,2,1:T(8,128)}), (f32[8,4,4,2,256]{4,3,2,1,0:T(2,128)}, f32[256,4,32]{0,2,1:T(8,128)})) %all-reduce.15.cloned.1.call-update) | async-done | bytes 393232 | tf_op jit(solution)/shard_map/psum | solution.py:171
  398.3 1.1 copy.213
  399.4 1.0 reshape.618
  400.4 9.9 %all-to-all-start.1 = ((f32[32,1,1024]{2,1,0:T(1,128)}), f32[32,1,1024]{2,1,0:T(1,128)S(1)}, u32[]{:S(2)}, u32[]{:S(2)}) async-start(f32[32,1,1024]{2,1,0:T(1,128)} %reshape.618), calls=%async_computation.1 | async-start | bytes 262144 | tf_op jit(solution)/shard_map/all_to_all | solution.py:111
  411.2 1.0 gather_fusion.1
  412.2 7.5 all-to-all-done.1
  419.7 1.0 reduce.6
  421.4 1.0 gather_fusion
  423.7 1.3 copy.250
  425.0 2.3 reshape.620
  427.3 12.7 %all_to_all.54 = bf16[32,2,1024]{2,1,0:T(2,128)(2,1)S(1)} all-to-all(bf16[32,2,1024]{2,1,0:T(2,128)(2,1)S(1)} %reshape.620), channel_id=1, replica_groups=mesh['gx'=16,'gy'=32] {'gy'}, dimensions={0} | all-to-all | bytes 262144 | tf_op jit(solution)/shard_map/all_to_all | solution.py:181
  440.0 2.4 reshape.621
  442.5 2.1 copy.252
  444.6 1.3 fusion.16
  446.0 37.6 %all_gather.9 = bf16[256,4,144]{2,1,0:T(4,128)(2,1)S(1)} all-gather(bf16[8,4,144]{2,1,0:T(4,128)(2,1)S(1)} %copy-done.2), channel_id=1, replica_groups=mesh['gx'=16,'gy'=32] {'gy'}, dimensions={0}, use_global_device_ids=true | all-gather | bytes 304128 | tf_op jit(solution)/shard_map/all_gather | solution.py:187
  483.6 115.7 %all-reduce.11.cloned.1.call-done = f32[256,4,144]{2,0,1:T(8,128)} async-done(((f32[256,4,144]{2,0,1:T(8,128)}), f32[256,4,144]{2,0,1:T(8,128)}) %all-reduce.11.cloned.1.call-update) | async-done | bytes 589840 | tf_op jit(solution)/shard_map/psum | solution.py:186
  599.3 1.4 multiply_reduce_fusion.1
  600.8 28.1 %psum.77 = f32[256,4]{0,1:T(4,128)S(1)} all-reduce(f32[256,4]{0,1:T(4,128)S(1)} %multiply_reduce_fusion.1), channel_id=1, replica_groups=mesh['gx'=16,'gy'=32] {'gx'}, use_global_device_ids=true, to_apply=%region_15.17 | all-reduce | flops 1024 | bytes 8192 | tf_op jit(solution)/shard_map/psum | solution.py:188
  628.9 1.6 multiply_reduce_fusion
  630.5 23.6 %psum.78 = f32[256,4]{0,1:T(4,128)S(1)} all-reduce(f32[256,4]{0,1:T(4,128)S(1)} %get-tuple-element.12), channel_id=1, replica_groups=mesh['gx'=16,'gy'=32] {'gx'}, use_global_device_ids=true, to_apply=%region_17.19 | all-reduce | flops 1024 | bytes 8192 | tf_op jit(solution)/shard_map/psum | solution.py:192
  655.9 1.6 pad_maximum_fusion
  657.4 2.1 copy.232
  659.5 1.9 reshape.525
  661.5 3.4 copy.233
  665.0 57.8 %reduce-scatter.2.cloned.1.call-done = f32[16,4,576]{2,0,1:T(8,128)} async-done(((f32[256,4,576]{2,0,1:T(8,128)}), f32[16,4,576]{2,0,1:T(8,128)}) %reduce-scatter.2.cloned.1.call-update) | async-done | bytes 147472 | tf_op jit(solution)/shard_map/reduce_scatter | solution.py:208
  722.8 1.1 fusion.31
  723.8 19.0 %all_gather.11 = bf16[256,4,288]{2,0,1:T(8,128)(2,1)S(1)} all-gather(bf16[16,4,288]{2,0,1:T(8,128)(2,1)S(1)} %fusion.31), channel_id=1, replica_groups=mesh['gx'=16,'gy'=32] {'gx'}, dimensions={0}, use_global_device_ids=true | all-gather | bytes 626688 | tf_op jit(solution)/shard_map/all_gather | solution.py:218
  743.3 1.7 copy.234
  745.0 1.3 dynamic-slice
  746.9 153.2 %all-reduce.13.cloned.1.call-done = f32[256,4,144]{2,1,0:T(4,128)} async-done(((f32[256,4,144]{2,1,0:T(4,128)}), f32[256,4,144]{2,1,0:T(4,128)}) %all-reduce.13.cloned.1.call-update) | async-done | bytes 589840
  900.1 0.8 multiply_reduce_fusion.3
  901.0 28.1 %psum.79 = f32[8,4]{0,1:T(4,128)S(1)} all-reduce(f32[8,4]{0,1:T(4,128)S(1)} %copy.235), channel_id=1, replica_groups=mesh['gx'=16,'gy'=32] {'gx'}, use_global_device_ids=true, to_apply=%region_21.23 | all-reduce | flops 32 | bytes 256 | tf_op jit(solution)/shard_map/psum | solution.py:223
  929.1 0.8 fusion.41
  930.0 0.6 copy.237
  (96 shorter events, 8.3 us)
Async XLA Ops:
  6.5 648.6 %copy-start = (bf16[144,288]{1,0:T(8,128)(2,1)S(1)}, bf16[144,288]{1,0:T(8,128)(2,1)}, u32[]{:S(2)}) copy-start(bf16[144,288]{1,0:T(8,128)(2,1)} %param.25) | copy-start | bytes 248836
  6.5 189.0 %all-reduce.9.cloned.1.call-start = ((), (), s32[]{:S(2)}) async-start(), calls=%async_computation.5 | async-start | bytes 524288 | tf_op jit(solution)/shard_map/psum | solution.py:106
  79.1 1.8 copy-start.8
  80.9 3.3 copy-start.6
  198.0 21.1 %all-to-all-start = ((f32[32,1,2048]{2,1,0:T(1,128)}), f32[32,1,2048]{2,1,0:T(1,128)S(1)}, u32[]{:S(2)}, u32[]{:S(2)}) async-start(f32[32,1,2048]{2,1,0:T(1,128)} %reshape.614), calls=%async_computation | async-start | bytes 524288 | tf_op jit(solution)/shard_map/all_to_all | solution.py:110
  208.5 2.1 copy-start.7
  273.5 126.9 %all-to-all-start.2 = ((bf16[32,2,512]{2,1,0:T(2,128)(2,1)}), bf16[32,2,512]{2,1,0:T(2,128)(2,1)S(1)}, u32[]{:S(2)}, u32[]{:S(2)}) async-start(bf16[32,2,512]{2,1,0:T(2,128)(2,1)} %reshape.616), calls=%async_computation.2 | async-start | bytes 131072 | tf_op jit(solution)/shard_map/all_to_all | solution.py:112
  277.3 121.0 %all-reduce.15.cloned.1.call-start = ((), (), s32[]{:S(2)}) async-start(), calls=%async_computation.9 | async-start | bytes 786432 | tf_op jit(solution)/shard_map/psum | solution.py:171
  400.4 19.3 %all-to-all-start.1 = ((f32[32,1,1024]{2,1,0:T(1,128)}), f32[32,1,1024]{2,1,0:T(1,128)S(1)}, u32[]{:S(2)}, u32[]{:S(2)}) async-start(f32[32,1,1024]{2,1,0:T(1,128)} %reshape.618), calls=%async_computation.1 | async-start | bytes 262144 | tf_op jit(solution)/shard_map/all_to_all | solution.py:111
  410.3 189.0 %all-reduce.11.cloned.1.call-start = ((), (), s32[]{:S(2)}) async-start(), calls=%async_computation.6 | async-start | bytes 2097152 | tf_op jit(solution)/shard_map/psum | solution.py:186
  421.3 2.0 copy-start.9
  440.0 4.6 copy-start.5
  442.5 3.5 copy-start.2
  445.9 276.8 %reduce-scatter.2.cloned.1.call-start = ((), (), s32[]{:S(2)}) async-start(), calls=%async_computation.7 | async-start | bytes 2785280 | tf_op jit(solution)/shard_map/reduce_scatter | solution.py:208
  630.5 23.8 %copy-start.1 = (f32[256,4,144]{2,0,1:T(8,128)}, f32[256,4,144]{2,0,1:T(8,128)S(1)}, u32[]{:S(2)}) copy-start(f32[256,4,144]{2,0,1:T(8,128)S(1)} %get-tuple-element.13) | copy-start | bytes 1769476
  654.3 1.1 copy-start.3
  664.9 77.9 %copy-start.4 = (bf16[288,144]{0,1:T(8,128)(2,1)S(1)}, bf16[288,144]{0,1:T(8,128)(2,1)}, u32[]{:S(2)}) copy-start(bf16[288,144]{0,1:T(8,128)(2,1)} %param.27) | copy-start | bytes 248836
  664.9 235.2 %all-reduce.13.cloned.1.call-start = ((), (), s32[]{:S(2)}) async-start(), calls=%async_computation.8 | async-start | bytes 2097152
Sparse Core Ops, SparseCore 0:
  76.6 118.8 all-reduce.8
  280.7 117.4 all-reduce.14
  446.0 153.2 all-reduce.10
  665.0 57.6 reduce-scatter.1
  745.1 154.9 all-reduce.12
where the time goes:
time: 938 us; the launch traced here: 937 us
  waiting for transfers between devices  574 us (61%)
  blocking collectives  262 us (28%)
  local copies, waits for them, and re-layouts  38.9 us (4%)
  starting transfers between devices  24 us (3%)
  between operations  15 us (2%)
  other arithmetic  14.8 us (2%)
    unnamed x6, waiting for transfers between devices  154 us
    psum x1, waiting for transfers between devices, body(): total_num, total_den = lax.psum((group_num, group_den), 'gx')  120 us
    psum x1, waiting for transfers between devices, body(): attn_full = lax.psum(attn_part, 'gy')  116 us
    psum x1, waiting for transfers between devices, body(): lax.psum((project(w_query), project(w_key), project(w_value)), 'gx')  111 us
    reduce_scatter x1, waiting for transfers between devices, body(): lax.psum_scatter(gate_and_up.reshape(ff_input.shape[0], steps_count, 2 *...  57.8 us
    psum x1, blocking collectives, body(): lax.psum((project(w_query), project(w_key), project(w_value)), 'gx')  47.4 us
    all_gather x1, blocking collectives, body(): lax.all_gather(inputs, 'gy', axis=0, tiled=True).astype(jnp.float32)  37.6 us
    all_gather x1, blocking collectives, body(): normed = lax.all_gather(normed_share, 'gy', axis=0, tiled=True)  36.1 us
  transfers between devices with their start and end apart: 8, of which 7 were waited for; matrix products, arithmetic and copies ran while one was open for 2% of the time, Pallas kernels for 0%

commit v1 on v0

--- a/solution.py
+++ b/solution.py
@@ -1,3 +1,4 @@
+import functools
 import jax
 import jax.numpy as jnp
 from jax import lax
@@ -13,6 +14,34 @@
 EPSILON = 1e-06
 SOFT_CAP = 50.0
 ROPE_BASE = 10000.0
+
+
+def treat_sheet(incoming_x, named_axis):
+    carry = jax.lax.psum(1, named_axis)
+    fresh = jax.lax.axis_index(named_axis)
+    v_next, work_now, placed = (carry, fresh, incoming_x.shape[0])
+    steps_seen = [(tick, (tick + 1) % v_next) for tick in range(v_next)]
+    table = [(tick, (tick - 1) % v_next) for tick in range(v_next)]
+    side_arr = jnp.zeros(
+        (*incoming_x.shape[:0], v_next * placed, *incoming_x.shape[1:]), incoming_x.dtype
+    )
+    frame_out = current_arr = incoming_x
+    current_value = v_next // 2
+    side_arr = lax.dynamic_update_slice_in_dim(side_arr, incoming_x, work_now * placed, axis=0)
+    for dev_j in range(1, current_value + 1):
+        frame_out = jax.lax.ppermute(frame_out, named_axis, steps_seen)
+        side_arr = lax.dynamic_update_slice_in_dim(
+            side_arr, frame_out, (work_now - dev_j) % v_next * placed, axis=0
+        )
+        if dev_j < v_next - current_value:
+            current_arr = jax.lax.ppermute(current_arr, named_axis, table)
+            side_arr = lax.dynamic_update_slice_in_dim(
+                side_arr, current_arr, (work_now + dev_j) % v_next * placed, axis=0
+            )
+    return side_arr
+
+
+wait_steps_all_by_axis = functools.partial(treat_sheet, named_axis="gx")
 
 
 def rotate(values, positions):
@@ -215,7 +244,7 @@
         jax.nn.gelu(activate_gate_and_up[..., :gate_width], approximate=True)
         * activate_gate_and_up[..., gate_width:]
     ).astype(jnp.bfloat16)
-    hidden_rows = lax.all_gather(hidden_share, "gx", axis=0, tiled=True)
+    hidden_rows = wait_steps_all_by_axis(hidden_share)
     down_part = jnp.dot(
         hidden_rows.reshape(-1, gate_width), w_down, preferred_element_type=jnp.float32
     ).reshape(hidden_rows.shape[0], steps_count, width_part)

time: 938 us -> 1060 us (1.13)
  waiting for transfers between devices: 574 us -> 643 us
  local copies, waits for them, and re-layouts: 38.9 us -> 76 us
  starting transfers between devices: 24 us -> 49 us
  blocking collectives: 262 us -> 243 us
    unnamed x6 -> x7, waiting for transfers between devices: 154 us -> 276 us
    reduce_scatter x1 -> x0, waiting for transfers between devices: 57.8 us -> none  [body(): lax.psum_scatter(gate_and_up.reshape(ff_input.shape[0], steps_count, 2 *...]
    dynamic_update_slice x0 -> x16, local copies, waits for them, and re-layouts: none -> 35.2 us  [the longest x8 16.7 us: treat_sheet(): lax.dynamic_update_slice_in_dim(side_arr, frame_out, (work_now - dev_j) %...]
    ppermute x0 -> x15, starting transfers between devices: none -> 24.8 us  [the longest x7 22.6 us: treat_sheet(): current_arr = jax.lax.ppermute(current_arr, named_axis, table)]
    all_gather x1 -> x0, blocking collectives: 19 us -> none  [body(): hidden_rows = lax.all_gather(hidden_share, 'gx', axis=0, tiled=True)]
  transfers between devices with their start and end apart: 8 -> 23, of which waited for: 7 -> 18; matrix products, arithmetic and copies ran while one was open for 2% -> 5% of each run, Pallas kernels for 0% -> 0%
where the time goes in v1:
time: 1060 us; the launch traced here: 1050 us
  waiting for transfers between devices  643 us (61%)
  blocking collectives  243 us (23%)
  local copies, waits for them, and re-layouts  76 us (7%)
  starting transfers between devices  49 us (5%)
  between operations  16.2 us (2%)
  other arithmetic  13.8 us (1%)
    unnamed x7, waiting for transfers between devices  276 us
    psum x1, waiting for transfers between devices, body(): total_num, total_den = lax.psum((group_num, group_den), 'gx')  120 us
    psum x1, waiting for transfers between devices, body(): attn_full = lax.psum(attn_part, 'gy')  116 us
    psum x1, waiting for transfers between devices, body(): lax.psum((project(w_query), project(w_key), project(w_value)), 'gx')  111 us
    psum x1, blocking collectives, body(): lax.psum((project(w_query), project(w_key), project(w_value)), 'gx')  47.3 us
    all_gather x1, blocking collectives, body(): lax.all_gather(inputs, 'gy', axis=0, tiled=True).astype(jnp.float32)  37.7 us
    all_gather x1, blocking collectives, body(): normed = lax.all_gather(normed_share, 'gy', axis=0, tiled=True)  36.1 us
    psum x1, blocking collectives, body(): square_sum = lax.psum(jnp.sum(x_wide * x_wide, axis=-1), 'gx')  29.8 us
  transfers between devices with their start and end apart: 23, of which 18 were waited for; matrix products, arithmetic and copies ran while one was open for 5% of the time, Pallas kernels for 0%

profile of v1, /device:TPU:1, one launch (start us, length us, event | category | flops | bytes accessed | tf_op | source)
XLA Modules:
  0.0 1050.3 jit_solution(2087379168428799380)
XLA Ops:
  8.1 29.8 %psum.70 = f32[8,4]{0,1:T(4,128)S(1)} all-reduce(f32[8,4]{0,1:T(4,128)S(1)} %fusion.33), channel_id=1, replica_groups=mesh['gx'=16,'gy'=32] {'gx'}, use_global_device_ids=true, to_apply=%region_3.0 | all-reduce | flops 32 | bytes 256 | tf_op jit(solution)/shard_map/psum | solution.py:122
  38.6 36.1 %all_gather.7 = bf16[256,4,144]{2,0,1:T(8,128)(2,1)S(1)} all-gather(bf16[8,4,144]{2,0,1:T(8,128)(2,1)S(1)} %fusion.35), channel_id=1, replica_groups=mesh['gx'=16,'gy'=32] {'gy'}, dimensions={0}, use_global_device_ids=true | all-gather | bytes 304128 | tf_op jit(solution)/shard_map/all_gather | solution.py:126
  74.7 1.7 fusion.37
  79.1 1.8 fusion.65
  84.7 110.9 %all-reduce.11.cloned.1.call-done = f32[256,4,64]{0,2,1:T(8,128)} async-done(((f32[256,4,64]{0,2,1:T(8,128)}), f32[256,4,64]{0,2,1:T(8,128)}) %all-reduce.11.cloned.1.call-update) | async-done | bytes 262160 | tf_op jit(solution)/shard_map/psum | solution.py:135
  195.6 1.2 copy.294
  196.8 1.2 reshape.615
  198.0 9.9 all-to-all-start
  208.5 1.3 copy.360
  211.6 7.5 all-to-all-done
  219.6 1.3 reduce.5
  221.9 1.7 fusion.67
  225.1 47.3 %all-reduce.20 = (bf16[256,4,32]{0,2,1:T(8,128)(2,1)S(1)}, f32[8,4,4,2]{0,2,3,1:T(4,128)S(1)}) all-reduce(f32[256,4,32]{0,2,1:T(8,128)S(1)} %fusion.42, f32[8,4,4,2]{0,2,3,1:T(4,128)S(1)} %copy.313), channel_id=1, replica_groups=mesh['gx'=16,'gy'=32] {'gx'}, use_global_device_ids=true, to_apply=%region_8.10 | all-reduce | flops 33024 | bytes 198656 | tf_op jit(solution)/shard_map/psum | solution.py:135
  273.5 3.8 all-to-all-start.2
  278.1 120.2 %all-reduce.19.cloned.1.call-done = (f32[8,4,4,2,256]{4,3,2,1,0:T(2,128)}, f32[256,4,32]{0,2,1:T(8,128)}) async-done(((f32[8,4,4,2,256]{4,3,2,1,0:T(2,128)}, f32[256,4,32]{0,2,1:T(8,128)}), (f32[8,4,4,2,256]{4,3,2,1,0:T(2,128)}, f32[256,4,32]{0,2,1:T(8,128)})) %all-reduce.19.cloned.1.call-update) | async-done | bytes 393232 | tf_op jit(solution)/shard_map/psum | solution.py:200
  398.3 1.1 copy.303
  400.4 9.9 all-to-all-start.1
  412.5 7.2 all-to-all-done.1
  423.7 1.3 copy.357
  425.0 2.3 reshape.621
  427.3 12.7 %all_to_all.54 = bf16[32,2,1024]{2,1,0:T(2,128)(2,1)S(1)} all-to-all(bf16[32,2,1024]{2,1,0:T(2,128)(2,1)S(1)} %reshape.621), channel_id=1, replica_groups=mesh['gx'=16,'gy'=32] {'gy'}, dimensions={0} | all-to-all | bytes 262144 | tf_op jit(solution)/shard_map/all_to_all | solution.py:210
  440.0 2.4 reshape.622
  442.5 2.1 copy.359
  444.6 1.3 fusion.16
  446.0 37.7 %all_gather.6 = bf16[256,4,144]{2,1,0:T(4,128)(2,1)S(1)} all-gather(bf16[8,4,144]{2,1,0:T(4,128)(2,1)S(1)} %copy-done.2), channel_id=1, replica_groups=mesh['gx'=16,'gy'=32] {'gy'}, dimensions={0}, use_global_device_ids=true | all-gather | bytes 304128 | tf_op jit(solution)/shard_map/all_gather | solution.py:216
  483.7 115.7 %all-reduce.13.cloned.1.call-done = f32[256,4,144]{2,0,1:T(8,128)} async-done(((f32[256,4,144]{2,0,1:T(8,128)}), f32[256,4,144]{2,0,1:T(8,128)}) %all-reduce.13.cloned.1.call-update) | async-done | bytes 589840 | tf_op jit(solution)/shard_map/psum | solution.py:215
  599.3 1.4 multiply_reduce_fusion.1
  600.8 28.1 %psum.77 = f32[256,4]{0,1:T(4,128)S(1)} all-reduce(f32[256,4]{0,1:T(4,128)S(1)} %multiply_reduce_fusion.1), channel_id=1, replica_groups=mesh['gx'=16,'gy'=32] {'gx'}, use_global_device_ids=true, to_apply=%region_15.17 | all-reduce | flops 1024 | bytes 8192 | tf_op jit(solution)/shard_map/psum | solution.py:217
  628.9 1.6 multiply_reduce_fusion
  630.5 23.6 %psum.78 = f32[256,4]{0,1:T(4,128)S(1)} all-reduce(f32[256,4]{0,1:T(4,128)S(1)} %get-tuple-element.12), channel_id=1, replica_groups=mesh['gx'=16,'gy'=32] {'gx'}, use_global_device_ids=true, to_apply=%region_17.19 | all-reduce | flops 1024 | bytes 8192 | tf_op jit(solution)/shard_map/psum | solution.py:221
  655.9 1.6 pad_maximum_fusion
  657.4 2.1 copy.322
  659.5 1.9 reshape.525
  661.5 1.3 dynamic-slice
  663.5 116.8 %all-reduce.15.cloned.1.call-done = f32[256,4,576]{2,1,0:T(4,128)} async-done(((f32[256,4,576]{2,1,0:T(4,128)}), f32[256,4,576]{2,1,0:T(4,128)}) %all-reduce.15.cloned.1.call-update) | async-done | bytes 2359312
  780.3 1.1 constant_dynamic-slice_fusion
  781.6 1.2 collective-permute-start.1
  783.5 1.6 collective-permute-start.2
  785.1 2.4 collective-permute-start.3
  788.6 3.6 collective-permute-start.5
  793.1 3.8 collective-permute-start.7
  797.9 3.8 collective-permute-start.9
  802.6 3.8 collective-permute-start.11
  807.3 3.8 collective-permute-start.13
  812.1 2.6 dynamic_update_slice.48
  814.9 1.3 dynamic_update_slice.49
  816.4 2.4 dynamic_update_slice.50
  819.1 2.2 dynamic_update_slice.51
  821.4 2.4 dynamic_update_slice.52
  824.1 2.2 dynamic_update_slice.53
  826.5 2.4 dynamic_update_slice.54
  829.1 2.2 dynamic_update_slice.55
  831.5 2.4 dynamic_update_slice.56
  834.1 2.2 dynamic_update_slice.57
  836.5 2.4 dynamic_update_slice.58
  839.2 2.2 dynamic_update_slice.59
  841.6 2.7 dynamic_update_slice.60
  844.4 2.2 dynamic_update_slice.61
  846.8 1.1 dynamic_update_slice.62
  848.1 2.2 dynamic_update_slice.63
  850.8 1.7 copy.341
  852.5 1.3 dynamic-slice.2
  854.4 158.6 %all-reduce.17.cloned.1.call-done = f32[256,4,144]{2,1,0:T(4,128)} async-done(((f32[256,4,144]{2,1,0:T(4,128)}), f32[256,4,144]{2,1,0:T(4,128)}) %all-reduce.17.cloned.1.call-update) | async-done | bytes 589840
  1014.0 28.1 %psum.79 = f32[8,4]{0,1:T(4,128)S(1)} all-reduce(f32[8,4]{0,1:T(4,128)S(1)} %copy.342), channel_id=1, replica_groups=mesh['gx'=16,'gy'=32] {'gx'}, use_global_device_ids=true, to_apply=%region_21.23 | all-reduce | flops 32 | bytes 256 | tf_op jit(solution)/shard_map/psum | solution.py:252
  (159 shorter events, 35.9 us)
Async XLA Ops:
  6.5 648.6 %copy-start = (bf16[144,288]{1,0:T(8,128)(2,1)S(1)}, bf16[144,288]{1,0:T(8,128)(2,1)}, u32[]{:S(2)}) copy-start(bf16[144,288]{1,0:T(8,128)(2,1)} %param.25) | copy-start | bytes 248836
  6.5 189.0 %all-reduce.11.cloned.1.call-start = ((), (), s32[]{:S(2)}) async-start(), calls=%async_computation.4 | async-start | bytes 524288 | tf_op jit(solution)/shard_map/psum | solution.py:135
  79.1 1.8 copy-start.8
  81.0 3.3 copy-start.6
  198.0 21.1 %all-to-all-start = ((f32[32,1,2048]{2,1,0:T(1,128)}), f32[32,1,2048]{2,1,0:T(1,128)S(1)}, u32[]{:S(2)}, u32[]{:S(2)}) async-start(f32[32,1,2048]{2,1,0:T(1,128)} %reshape.615), calls=%async_computation | async-start | bytes 524288 | tf_op jit(solution)/shard_map/all_to_all | solution.py:139
  208.5 2.1 copy-start.7
  273.5 126.9 %all-to-all-start.2 = ((bf16[32,2,512]{2,1,0:T(2,128)(2,1)}), bf16[32,2,512]{2,1,0:T(2,128)(2,1)S(1)}, u32[]{:S(2)}, u32[]{:S(2)}) async-start(bf16[32,2,512]{2,1,0:T(2,128)(2,1)} %reshape.617), calls=%async_computation.2 | async-start | bytes 131072 | tf_op jit(solution)/shard_map/all_to_all | solution.py:141
  277.3 121.0 %all-reduce.19.cloned.1.call-start = ((), (), s32[]{:S(2)}) async-start(), calls=%async_computation.8 | async-start | bytes 786432 | tf_op jit(solution)/shard_map/psum | solution.py:200
  400.4 19.3 %all-to-all-start.1 = ((f32[32,1,1024]{2,1,0:T(1,128)}), f32[32,1,1024]{2,1,0:T(1,128)S(1)}, u32[]{:S(2)}, u32[]{:S(2)}) async-start(f32[32,1,1024]{2,1,0:T(1,128)} %reshape.619), calls=%async_computation.1 | async-start | bytes 262144 | tf_op jit(solution)/shard_map/all_to_all | solution.py:140
  410.3 189.0 %all-reduce.13.cloned.1.call-start = ((), (), s32[]{:S(2)}) async-start(), calls=%async_computation.5 | async-start | bytes 2097152 | tf_op jit(solution)/shard_map/psum | solution.py:215
  421.3 2.0 copy-start.9
  440.0 4.6 copy-start.5
  442.5 3.5 copy-start.2
  445.9 334.4 %all-reduce.15.cloned.1.call-start = ((), (), s32[]{:S(2)}) async-start(), calls=%async_computation.6 | async-start | bytes 5242880
  630.5 23.8 %copy-start.1 = (f32[256,4,144]{2,0,1:T(8,128)}, f32[256,4,144]{2,0,1:T(8,128)S(1)}, u32[]{:S(2)}) copy-start(f32[256,4,144]{2,0,1:T(8,128)S(1)} %get-tuple-element.13) | copy-start | bytes 1769476
  654.3 1.1 copy-start.3
  661.5 351.5 %all-reduce.17.cloned.1.call-start = ((), (), s32[]{:S(2)}) async-start(), calls=%async_computation.7 | async-start | bytes 2097152
  781.4 2.1 collective-permute-start
  781.6 3.5 collective-permute-start.1
  783.5 4.7 collective-permute-start.2
  785.1 3.5 collective-permute-start.3
  788.2 4.7 collective-permute-start.4
  788.6 4.5 collective-permute-start.5
  793.0 4.7 collective-permute-start.6
  793.1 4.7 collective-permute-start.7
  797.7 4.7 collective-permute-start.8
  797.9 4.7 collective-permute-start.9
  802.4 4.7 collective-permute-start.10
  802.6 4.7 collective-permute-start.11
  807.1 4.7 collective-permute-start.12
  807.3 39.3 %collective-permute-start.13 = (bf16[16,4,288]{2,0,1:T(8,128)(2,1)S(1)}, bf16[16,4,288]{2,0,1:T(8,128)(2,1)S(1)}, u32[]{:S(2)}, u32[]{:S(2)}) collective-permute-start(bf16[16,4,288]{2,0,1:T(8,128)(2,1)S(1)} %collective-permute-done.11), channel_id=1, source_target_pairs={{0,480},{32,0},{64,32},{96,64},{128,96},{160,128},{192,160},{224,1... | collective-permute-start | bytes 110600 | tf_op jit(solution)/shard_map/ppermute | solution.py:37
  811.9 36.0 %collective-permute-start.14 = (bf16[16,4,288]{2,0,1:T(8,128)(2,1)S(1)}, bf16[16,4,288]{2,0,1:T(8,128)(2,1)S(1)}, u32[]{:S(2)}, u32[]{:S(2)}) collective-permute-start(bf16[16,4,288]{2,0,1:T(8,128)(2,1)S(1)} %collective-permute-done.12), channel_id=1, source_target_pairs={{0,32},{32,64},{64,96},{96,128},{128,160},{160,192},{192,224},{224... | collective-permute-start | bytes 110600 | tf_op jit(solution)/shard_map/ppermute | solution.py:32
  839.2 11.1 %copy-start.4 = (bf16[288,144]{0,1:T(8,128)(2,1)S(1)}, bf16[288,144]{0,1:T(8,128)(2,1)}, u32[]{:S(2)}) copy-start(bf16[288,144]{0,1:T(8,128)(2,1)} %param.27) | copy-start | bytes 248836
Sparse Core Ops, SparseCore 0:
  76.6 118.8 all-reduce.10
  280.7 117.5 all-reduce.18
  446.0 153.2 all-reduce.12
  661.6 118.6 all-reduce.14
  852.6 160.3 all-reduce.16
